TPU v7x, 32 devices: a whole 2x2x4 slice. The times are simulated.
32 devices in a mesh: dp: 2 (over x), row: 4 (over y, core), col: 4 (over z).
Axes of the slice: x: 2, y: 2, z: 4, core: 2. Of those that a mesh axis runs over, the one named last changes fastest.
Arguments:
- tokens: bfloat16 [768, 39200], P('row', ('dp', 'col')), may hold values from -6 to 6
- grad_out: bfloat16 [768, 39200], P('row', ('dp', 'col')), may hold values from -6 to 6
- adapter_index: int32 [8, 1], replicated, may hold values from 0 to 7
- norm1_gain: bfloat16 [768], P('row'), may hold values from 0.099609375 to 1.8984375
- norm2_gain: bfloat16 [768], P('row'), may hold values from 0.099609375 to 1.8984375
- qkv_weight: bfloat16 [768, 2304], P('row', 'col'), may hold values from -0.21875 to 0.21875
- proj_weight: bfloat16 [768, 768], P('col', 'row'), may hold values from -0.875 to 0.875
- fc1_weight: bfloat16 [768, 3072], P('row', 'col'), may hold values from -0.21875 to 0.21875
- fc2_weight: bfloat16 [768, 3072], P('row', 'col'), may hold values from -0.109375 to 0.109375
- rel_h: bfloat16 [27, 64], replicated, may hold values from -0.59765625 to 0.59765625
- rel_w: bfloat16 [27, 64], replicated, may hold values from -0.59765625 to 0.59765625
- qkv_down: bfloat16 [8, 768, 16], P(None, 'row'), may hold values from -0.21875 to 0.21875
- qkv_up: bfloat16 [8, 16, 2304], P(None, None, 'col'), may hold values from -0.75 to 0.75
- proj_down: bfloat16 [8, 768, 16], P(None, 'col'), may hold values from -0.21875 to 0.21875
- proj_up: bfloat16 [8, 16, 768], P(None, None, 'row'), may hold values from -0.75 to 0.75
- fc1_down: bfloat16 [8, 768, 16], P(None, 'row'), may hold values from -0.21875 to 0.21875
- fc1_up: bfloat16 [8, 16, 3072], P(None, None, 'col'), may hold values from -0.75 to 0.75
- fc2_down: bfloat16 [8, 3072, 16], P(None, 'col'), may hold values from -0.109375 to 0.109375
- fc2_up: bfloat16 [8, 16, 768], P(None, None, 'row'), may hold values from -0.75 to 0.75
Outputs:
- out: bfloat16 [768, 39200], P('row', ('dp', 'col'))
- tokens_grad: float32 [768, 39200], P('row', ('dp', 'col'))
- qkv_down_grad: float32 [8, 768, 16], P(None, 'row')
- qkv_up_grad: float32 [8, 16, 2304], P(None, None, 'col')
- proj_down_grad: float32 [8, 768, 16], P(None, 'col')
- proj_up_grad: float32 [8, 16, 768], P(None, None, 'row')
- fc1_down_grad: float32 [8, 768, 16], P(None, 'row')
- fc1_up_grad: float32 [8, 16, 3072], P(None, None, 'col')
- fc2_down_grad: float32 [8, 3072, 16], P(None, 'col')
- fc2_up_grad: float32 [8, 16, 768], P(None, None, 'row')
Inputs may be any that keep to these rules, and one draw needn't show every extreme that they name: `adapter_index`: every one of the 8 adapters is chosen by at least one image.
All inputs are finite; a program needn't handle non-finite values.
Results may differ from a plain program's by a relative error of at most 0.015.
Values may be sent and summed in bfloat16 or wider, within the bound.
No kernel may reach another device: no remote copies, remote signals or barrier semaphores. Data moves between devices by JAX's collectives and lax.ppermute only.
A program may use at most 448 MiB of HBM per device.

v0:
```python
import jax
import jax.numpy as jnp
from jax import lax
from jax.sharding import PartitionSpec as P

D = 768
HD = 64
WIN = 14
SIDE = 64
ADAPT = 8
NWIN_SIDE = 5
IMG_TOK = 4900
PRECISE = lax.Precision.HIGHEST
EPSILON = 1e-06


def exact_gelu(values):
    return jax.nn.gelu(values, approximate=False)


def valid_rows():
    position = jnp.arange(IMG_TOK, dtype=jnp.int32)
    window = position // (WIN * WIN)
    inside = position % (WIN * WIN)
    image_row = window // NWIN_SIDE * WIN + inside // WIN
    image_col = window % NWIN_SIDE * WIN + inside % WIN
    return ((image_row < SIDE) & (image_col < SIDE)).astype(jnp.float32)


def rel_table(rel_param):
    offsets = (
        jnp.arange(WIN, dtype=jnp.int32)[:, None]
        - jnp.arange(WIN, dtype=jnp.int32)[None, :]
        + WIN
        - 1
    )
    one_hot = (
        offsets[:, :, None] == jnp.arange(2 * WIN - 1, dtype=jnp.int32)[None, None, :]
    ).astype(jnp.bfloat16)
    return jnp.einsum("akn,nc->akc", one_hot, rel_param, preferred_element_type=jnp.float32).astype(
        jnp.bfloat16
    )


def pick_one(adapter, own_pick):
    return jnp.einsum("a,ade->de", own_pick, adapter.astype(jnp.float32), precision=PRECISE).astype(
        jnp.bfloat16
    )


def row_totals(first_sum, second_sum):
    return lax.psum((first_sum, second_sum), "row")


def norm_forward(values):
    totals = row_totals(jnp.sum(values, axis=1), jnp.sum(values * values, axis=1))
    center = totals[0] / D
    inv_std = lax.rsqrt(totals[1] / D - center * center + EPSILON)
    return ((values - center[:, None]) * inv_std[:, None], inv_std)


def norm_backward(grad_normed, normed, inv_std):
    totals = row_totals(jnp.sum(grad_normed, axis=1), jnp.sum(grad_normed * normed, axis=1))
    return inv_std[:, None] * (
        grad_normed - totals[0][:, None] / D - normed * totals[1][:, None] / D
    )


def local_norm(values):
    center = jnp.sum(values, axis=1) / D
    inv_std = lax.rsqrt(jnp.sum(values * values, axis=1) / D - center * center + EPSILON)
    return ((values - center[:, None]) * inv_std[:, None], inv_std)


def local_norm_back(grad_normed, normed, inv_std):
    first_mean = jnp.sum(grad_normed, axis=1) / D
    second_mean = jnp.sum(grad_normed * normed, axis=1) / D
    return inv_std[:, None] * (grad_normed - first_mean[:, None] - normed * second_mean[:, None])


def to_features(values):
    return lax.all_to_all(
        values.astype(jnp.bfloat16), "row", split_axis=0, concat_axis=1, tiled=True
    ).astype(values.dtype)


def to_tokens(values):
    return lax.all_to_all(
        values.astype(jnp.bfloat16), "row", split_axis=1, concat_axis=0, tiled=True
    ).astype(values.dtype)


def token_rows(values):
    return lax.all_to_all(values, "row", split_axis=0, concat_axis=1, tiled=True)


def head_cols(values):
    return lax.all_to_all(values, "row", split_axis=1, concat_axis=0, tiled=True)


def head_sums(values):
    return lax.all_to_all(
        values.astype(jnp.bfloat16), "row", split_axis=1, concat_axis=0, tiled=True
    ).astype(values.dtype)


def adapted_local(inputs, weight, down_mat, up_mat):
    product = jnp.dot(inputs, weight, preferred_element_type=jnp.float32)
    reduced = jnp.dot(inputs, down_mat, preferred_element_type=jnp.float32)
    return product + jnp.dot(reduced, up_mat.astype(jnp.float32), precision=PRECISE)


def adapted_back(grads, weight, down_mat, up_mat):
    contract = (((1,), (1,)), ((), ()))
    product = lax.dot_general(grads, weight, contract, preferred_element_type=jnp.float32)
    reduced = lax.dot_general(grads, up_mat, contract, preferred_element_type=jnp.float32)
    return product + lax.dot_general(
        reduced, down_mat.astype(jnp.float32), contract, precision=PRECISE
    )


def pair_grads(inputs_m, grads_m, down_m, up_m):
    reduced = jnp.dot(inputs_m, down_m, preferred_element_type=jnp.float32)
    back_red = lax.dot_general(
        grads_m, up_m, (((1,), (1,)), ((), ())), preferred_element_type=jnp.float32
    )
    grad_down = jnp.einsum("td,tr->dr", inputs_m, back_red, precision=PRECISE)
    grad_up = jnp.einsum("tr,to->ro", reduced, grads_m, precision=PRECISE)
    return (grad_down, grad_up)


def spread_pick(own_pick, grad_mat):
    return jnp.einsum("a,de->ade", own_pick, grad_mat)


def take_block(full, dim, index, length):
    return lax.dynamic_slice_in_dim(full, index * length, length, dim)


def split_qkv(qkv_low):
    heads_local = qkv_low.shape[1] // (3 * HD)
    arranged = qkv_low.reshape(NWIN_SIDE * NWIN_SIDE, WIN * WIN, heads_local, 3, HD)
    return (arranged[:, :, :, 0], arranged[:, :, :, 1], arranged[:, :, :, 2])


def score_matrix(query_b, key_b, tables):
    windows = query_b.shape[0]
    heads_local = query_b.shape[2]
    dot_scores = jnp.einsum(
        "nqhc,nkhc->nhqk", query_b, key_b, preferred_element_type=jnp.float32
    ) * HD ** (-0.5)
    spatial = query_b.reshape(windows, WIN, WIN, heads_local, HD)
    rel_rows = jnp.einsum(
        "nabhc,akc->nhabk", spatial, tables[0], preferred_element_type=jnp.float32
    )
    rel_cols = jnp.einsum(
        "nabhc,bkc->nhabk", spatial, tables[1], preferred_element_type=jnp.float32
    )
    shaped = dot_scores.reshape(windows, heads_local, WIN, WIN, WIN, WIN)
    shaped = shaped + rel_rows[:, :, :, :, :, None] + rel_cols[:, :, :, :, None, :]
    return shaped.reshape(windows, heads_local, WIN * WIN, WIN * WIN)


def attend(qkv_low, tables):
    query_b, key_b, value_b = split_qkv(qkv_low)
    scores = score_matrix(query_b, key_b, tables)
    maxima = jnp.max(scores, axis=3, keepdims=True)
    exponent = jnp.exp(scores - maxima)
    sum_exp = jnp.sum(exponent, axis=3, keepdims=True)
    attn_prob = (exponent / sum_exp).astype(jnp.bfloat16)
    attended = jnp.einsum("nhqk,nkhc->nqhc", attn_prob, value_b, preferred_element_type=jnp.float32)
    log_total = (maxima + jnp.log(sum_exp))[:, :, :, 0]
    return (attended.reshape(IMG_TOK, attended.shape[2] * HD).astype(jnp.bfloat16), log_total)


def attend_back(qkv_low, log_total, grad_attended, tables):
    query_b, key_b, value_b = split_qkv(qkv_low)
    windows = query_b.shape[0]
    heads_local = query_b.shape[2]
    scores = score_matrix(query_b, key_b, tables)
    attn_exact = jnp.exp(scores - log_total[:, :, :, None])
    prob_low = attn_exact.astype(jnp.bfloat16)
    grad_o = grad_attended.reshape(windows, WIN * WIN, heads_local, HD)
    grad_v = jnp.einsum("nhqk,nqhc->nkhc", prob_low, grad_o, preferred_element_type=jnp.float32)
    grad_p = jnp.einsum("nqhc,nkhc->nhqk", grad_o, value_b, preferred_element_type=jnp.float32)
    centre = jnp.sum(grad_p * attn_exact, axis=3, keepdims=True)
    grad_s = (attn_exact * (grad_p - centre)).astype(jnp.bfloat16)
    grad_q = jnp.einsum(
        "nhqk,nkhc->nqhc", grad_s, key_b, preferred_element_type=jnp.float32
    ) * HD ** (-0.5)
    grad_k = jnp.einsum(
        "nhqk,nqhc->nkhc", grad_s, query_b, preferred_element_type=jnp.float32
    ) * HD ** (-0.5)
    split_grad = grad_s.astype(jnp.float32).reshape(windows, heads_local, WIN, WIN, WIN, WIN)
    along_rows = jnp.sum(split_grad, axis=5)
    along_cols = jnp.sum(split_grad, axis=4)
    rel_grad = jnp.einsum(
        "nhabk,akc->nabhc", along_rows, tables[0].astype(jnp.float32), precision=PRECISE
    )
    rel_grad = rel_grad + jnp.einsum(
        "nhabk,bkc->nabhc", along_cols, tables[1].astype(jnp.float32), precision=PRECISE
    )
    grad_q = grad_q + rel_grad.reshape(windows, WIN * WIN, heads_local, HD)
    stacked = jnp.stack([grad_q, grad_k, grad_v], axis=3)
    return stacked.reshape(IMG_TOK, heads_local * 3 * HD).astype(jnp.bfloat16)


def body(
    tokens,
    grad_out,
    adapter_index,
    norm1_gain,
    norm2_gain,
    qkv_weight,
    proj_weight,
    fc1_weight,
    fc2_weight,
    rel_h,
    rel_w,
    qkv_down,
    qkv_up,
    proj_down,
    proj_up,
    fc1_down,
    fc1_up,
    fc2_down,
    fc2_up,
):
    members = lax.axis_size("col")
    row_index = lax.axis_index("row")
    col_index = lax.axis_index("col")
    group_ids = lax.dynamic_slice_in_dim(
        adapter_index[:, 0], lax.axis_index("dp") * members, members, 0
    )
    chosen = (group_ids[:, None] == jnp.arange(ADAPT, dtype=jnp.int32)[None, :]).astype(jnp.float32)
    own_pick = chosen[col_index]
    validity = valid_rows()[:, None]
    tables = (rel_table(rel_h), rel_table(rel_w))
    inputs = tokens.astype(jnp.float32).T
    normed_one, inv_one = norm_forward(inputs)
    gain_one = norm1_gain.astype(jnp.float32)
    hidden_one = (normed_one * gain_one * validity).astype(jnp.bfloat16)
    qkv_part, proj_part, qkv_dn_part, proj_up_part = (
        lax.all_gather(qkv_weight, "row", axis=0, tiled=True),
        lax.all_gather(proj_weight, "row", axis=1, tiled=True),
        lax.all_gather(qkv_down, "row", axis=1, tiled=True),
        lax.all_gather(proj_up, "row", axis=2, tiled=True),
    )
    qkv_full, proj_full, qkv_up_all, proj_dn_all = (
        lax.all_gather(qkv_part, "col", axis=1, tiled=True),
        lax.all_gather(proj_part, "col", axis=0, tiled=True),
        lax.all_gather(qkv_up, "col", axis=2, tiled=True),
        lax.all_gather(proj_down, "col", axis=1, tiled=True),
    )
    qkv_dn = pick_one(qkv_dn_part, own_pick)
    qkv_upm = pick_one(qkv_up_all, own_pick)
    proj_dn = pick_one(proj_dn_all, own_pick)
    proj_upm = pick_one(proj_up_part, own_pick)
    hidden_rows = token_rows(hidden_one)
    qkv_rows_out = adapted_local(hidden_rows, qkv_full, qkv_dn, qkv_upm).astype(jnp.bfloat16)
    qkv_low = head_cols(qkv_rows_out)
    attended, log_total = attend(qkv_low, tables)
    attended_rows = token_rows(attended)
    branch = head_sums(adapted_local(attended_rows, proj_full, proj_dn, proj_upm))
    middle = inputs + branch
    grad_final = grad_out.astype(jnp.float32).T * validity
    weight_up, weight_stored, down_one, up_two, gain_full = (
        lax.all_gather(fc1_weight, "row", axis=0, tiled=True),
        lax.all_gather(fc2_weight, "row", axis=0, tiled=True),
        lax.all_gather(fc1_down, "row", axis=1, tiled=True),
        lax.all_gather(fc2_up, "row", axis=2, tiled=True),
        lax.all_gather(norm2_gain, "row", axis=0, tiled=True),
    )
    weight_up, weight_stored, up_one, down_two = (
        lax.all_gather(weight_up, "col", axis=1, tiled=True),
        lax.all_gather(weight_stored, "col", axis=1, tiled=True),
        lax.all_gather(fc1_up, "col", axis=2, tiled=True),
        lax.all_gather(fc2_down, "col", axis=1, tiled=True),
    )
    weight_down = weight_stored.T
    down_fc1 = pick_one(down_one, own_pick)
    up_fc1 = pick_one(up_one, own_pick)
    down_fc2 = pick_one(down_two, own_pick)
    up_fc2 = pick_one(up_two, own_pick)
    local_mid = to_features(middle)
    normed_two, inv_two = local_norm(local_mid)
    gain_two = gain_full.astype(jnp.float32)
    hidden_two = (normed_two * gain_two).astype(jnp.bfloat16)
    pre_act = adapted_local(hidden_two, weight_up, down_fc1, up_fc1)
    activated = exact_gelu(pre_act).astype(jnp.bfloat16)
    mlp_out = to_tokens(adapted_local(activated, weight_down, down_fc2, up_fc2))
    grad_local = to_features(grad_final).astype(jnp.bfloat16)
    grad_activ = adapted_back(grad_local, weight_down, down_fc2, up_fc2)
    gelu_value, gelu_back = jax.vjp(exact_gelu, pre_act)
    grad_pre = gelu_back(grad_activ)[0].astype(jnp.bfloat16)
    grad_hidden_two = adapted_back(grad_pre, weight_up, down_fc1, up_fc1)
    grad_middle = grad_final + to_tokens(
        local_norm_back(grad_hidden_two * gain_two, normed_two, inv_two)
    )
    fc1_local = pair_grads(hidden_two, grad_pre, down_fc1, up_fc1)
    fc2_local = pair_grads(activated, grad_local, down_fc2, up_fc2)
    summed_all = lax.psum(
        (
            spread_pick(own_pick, fc1_local[0]),
            spread_pick(own_pick, fc1_local[1]),
            spread_pick(own_pick, fc2_local[0]),
            spread_pick(own_pick, fc2_local[1]),
        ),
        ("dp", "row", "col"),
    )
    fc1_down_grad = take_block(summed_all[0], 1, row_index, fc1_down.shape[1])
    fc1_up_grad = take_block(summed_all[1], 2, col_index, fc1_up.shape[2])
    fc2_down_grad = take_block(summed_all[2], 1, col_index, fc2_down.shape[1])
    fc2_up_grad = take_block(summed_all[3], 2, row_index, fc2_up.shape[2])
    result = ((middle + mlp_out) * validity).astype(jnp.bfloat16).T
    grad_branch = grad_middle.astype(jnp.bfloat16)
    grad_branch_rows = token_rows(grad_branch)
    grad_attended = head_cols(
        adapted_back(grad_branch_rows, proj_full, proj_dn, proj_upm).astype(jnp.bfloat16)
    )
    grad_qkv = attend_back(qkv_low, log_total, grad_attended, tables)
    grad_qkv_rows = token_rows(grad_qkv)
    grad_hidden_one = head_sums(adapted_back(grad_qkv_rows, qkv_full, qkv_dn, qkv_upm))
    qkv_pair = pair_grads(hidden_rows, grad_qkv_rows, qkv_dn, qkv_upm)
    proj_pair = pair_grads(attended_rows, grad_branch_rows, proj_dn, proj_upm)
    attn_sums = lax.psum(
        (
            spread_pick(own_pick, qkv_pair[0]),
            spread_pick(own_pick, qkv_pair[1]),
            spread_pick(own_pick, proj_pair[0]),
            spread_pick(own_pick, proj_pair[1]),
        ),
        ("dp", "row", "col"),
    )
    qkv_down_grad = take_block(attn_sums[0], 1, row_index, qkv_down.shape[1])
    qkv_up_grad = take_block(attn_sums[1], 2, col_index, qkv_up.shape[2])
    proj_down_grad = take_block(attn_sums[2], 1, col_index, proj_down.shape[1])
    proj_up_grad = take_block(attn_sums[3], 2, row_index, proj_up.shape[2])
    grad_inputs = (
        grad_middle + norm_backward(grad_hidden_one * validity * gain_one, normed_one, inv_one)
    ).T
    return (
        result,
        grad_inputs,
        qkv_down_grad,
        qkv_up_grad,
        proj_down_grad,
        proj_up_grad,
        fc1_down_grad,
        fc1_up_grad,
        fc2_down_grad,
        fc2_up_grad,
    )


def solution(mesh):
    return jax.shard_map(
        body,
        mesh=mesh,
        in_specs=(
            P("row", ("dp", "col")),
            P("row", ("dp", "col")),
            P(),
            P("row"),
            P("row"),
            P("row", "col"),
            P("col", "row"),
            P("row", "col"),
            P("row", "col"),
            P(),
            P(),
            P(None, "row", None),
            P(None, None, "col"),
            P(None, "col", None),
            P(None, None, "row"),
            P(None, "row", None),
            P(None, None, "col"),
            P(None, "col", None),
            P(None, None, "row"),
        ),
        out_specs=(
            P("row", ("dp", "col")),
            P("row", ("dp", "col")),
            P(None, "row", None),
            P(None, None, "col"),
            P(None, "col", None),
            P(None, None, "row"),
            P(None, "row", None),
            P(None, None, "col"),
            P(None, "col", None),
            P(None, None, "row"),
        ),
        check_vma=False,
    )
```

profile of v0, /device:TPU:0, one launch (start us, length us, event | category | flops | bytes accessed | tf_op | source)
XLA Modules:
  0.0 1826.9 jit_solution(15166732212104624496)
XLA Ops:
  7.3 11.5 all_gather.51
  20.9 11.5 all-reduce.3
  46.7 118.0 %all_gather.54 = bf16[8,16,2304]{1,0,2:T(8,128)(2,1)} all-gather(bf16[8,16,576]{1,0,2:T(8,128)(2,1)S(1)} %copy.225), channel_id=1, replica_groups=mesh['dp'=2,'row'=4,'col'=4] {'col'}, dimensions={2}, use_global_device_ids=true | all-gather | bytes 737280 | tf_op jit(solution)/shard_map/all_gather | solution.py:252
  171.6 12.9 all_gather.62
  184.5 30.9 %all_gather.57 = bf16[8,768,16]{2,0,1:T(8,128)(2,1)S(1)} all-gather(bf16[8,192,16]{2,0,1:T(8,128)(2,1)} %copy.243), channel_id=1, replica_groups=mesh['dp'=2,'row'=4,'col'=4] {'col'}, dimensions={1}, use_global_device_ids=true | all-gather | bytes 245760 | tf_op jit(solution)/shard_map/all_gather | solution.py:253
  215.4 12.6 all_gather.53
  233.1 7.3 fusion.133
  240.4 7.2 fusion.8
  247.6 8.9 copy.226
  263.0 74.5 %all_gather.55 = bf16[192,768]{0,1:T(8,128)(2,1)S(1)} all-gather(bf16[192,192]{0,1:T(8,128)(2,1)S(1)} %copy.241), channel_id=1, replica_groups=mesh['dp'=2,'row'=4,'col'=4] {'row'}, dimensions={1}, use_global_device_ids=true | all-gather | bytes 368640 | tf_op jit(solution)/shard_map/all_gather | solution.py:245
  338.7 13.0 all_gather.58
  362.3 9.7 copy.227
  372.0 26.8 %reshape.211 = bf16[25,196,3,3,64]{1,0,4,3,2:T(8,128)(2,1)} reshape(bf16[4,1225,576]{1,0,2:T(4,128)(2,1)} %copy.227) | data formatting | bytes 11289600 | tf_op jit(solution)/shard_map/reshape | solution.py:142
  410.5 7.5 reshape_squeeze.4
  418.0 8.6 fusion.52
  427.1 21.4 %add.271 = f32[25,3,14,14,14,14]{0,5,4,3,2,1:T(8,128)} broadcast(f32[25,3,14,14,14]{0,4,3,2,1:T(8,128)S(1)} %copy.236), dimensions={0,1,2,3,5} | broadcast | bytes 12348000 | tf_op jit(solution)/shard_map/add | solution.py:160
  448.6 64.5 %add.272 = f32[25,3,196,196]{0,3,2,1:T(8,128)} reshape(f32[25,3,14,14,14,14]{0,5,4,3,2,1:T(8,128)} %add.271) | data formatting | bytes 23049600 | tf_op jit(solution)/shard_map/add | solution.py:160
  513.1 39.1 %copy.237 = f32[25,3,196,196]{2,3,1,0:T(8,128)} copy(f32[25,3,196,196]{0,3,2,1:T(8,128)} %add.272) | data formatting | bytes 23049600 | tf_op jit(solution)/shard_map/add | solution.py:160
  552.2 8.6 fusion.49
  563.4 22.8 %add.268 = f32[25,3,14,14,14,14]{0,5,4,3,2,1:T(8,128)} broadcast(f32[25,3,14,14,14]{0,4,3,2,1:T(8,128)} %copy.233), dimensions={0,1,2,3,4} | broadcast | bytes 12348000 | tf_op jit(solution)/shard_map/add | solution.py:160
  586.3 64.5 %add.269 = f32[25,3,196,196]{0,3,2,1:T(8,128)} reshape(f32[25,3,14,14,14,14]{0,5,4,3,2,1:T(8,128)} %add.268) | data formatting | bytes 23049600 | tf_op jit(solution)/shard_map/add | solution.py:160
  650.8 39.1 %copy.234 = f32[25,3,196,196]{2,3,1,0:T(8,128)} copy(f32[25,3,196,196]{0,3,2,1:T(8,128)} %add.269) | data formatting | bytes 23049600 | tf_op jit(solution)/shard_map/add | solution.py:160
  689.9 24.5 %fusion.132 = (f32[25,3,196]{2,1,0:T(4,128)S(1)}, f32[25,3,196,196]{2,3,1,0:T(8,128)}) fusion(f32[25,3,196,196]{2,3,1,0:T(8,128)} %copy.237, f32[25,3,196,196]{2,3,1,0:T(8,128)} %copy.234, bf16[25,196,3,1,64]{1,0,4,3,2:T(8,128)(2,1)} %get-tuple-element.37, bf16[25,196,3,1,64]{1,0,4,3,2:T(8,128)(2,1)S(1)} %copy-done.9), kind=kOutput, calls=%fused_computation.234 | convolution fusion | flops 380303744 | bytes 38396400 | tf_op jit(solution)/shard_map/nqhc,nkhc->nhqk/dot_general | solution.py:149
  714.4 9.8 fusion.6
  724.2 10.1 convert_bitcast_fusion.6
  735.9 7.6 convert_element_type.214
  763.8 10.6 all-to-all-done.2
  779.3 33.6 %all_gather.67 = bf16[8,16,768]{1,0,2:T(8,128)(2,1)S(1)} all-gather(bf16[8,16,192]{1,0,2:T(8,128)(2,1)} %copy.250), channel_id=1, replica_groups=mesh['dp'=2,'row'=4,'col'=4] {'row'}, dimensions={2}, use_global_device_ids=true | all-gather | bytes 245760 | tf_op jit(solution)/shard_map/all_gather | solution.py:271
  814.5 19.3 %all_gather.66 = bf16[8,3072,16]{1,2,0:T(8,128)(2,1)S(1)} all-gather(bf16[8,768,16]{1,2,0:T(8,128)(2,1)} %param.36), channel_id=1, replica_groups=mesh['dp'=2,'row'=4,'col'=4] {'col'}, dimensions={1}, use_global_device_ids=true | all-gather | bytes 983040 | tf_op jit(solution)/shard_map/all_gather | solution.py:278
  850.3 7.8 fusion.62
  858.0 9.8 copy.292
  868.1 30.2 %all_gather.63 = bf16[8,16,3072]{2,1,0:T(8,128)(2,1)S(1)} all-gather(bf16[8,16,768]{2,1,0:T(8,128)(2,1)S(1)} %copy-done.72), channel_id=1, replica_groups=mesh['dp'=2,'row'=4,'col'=4] {'col'}, dimensions={2}, use_global_device_ids=true | all-gather | bytes 983040 | tf_op jit(solution)/shard_map/all_gather | solution.py:277
  928.8 11.8 fusion.137
  940.6 12.5 all-to-all-done.4
  967.9 8.0 fusion.135
  975.9 41.4 %multiply_convert_fusion.1 = (bf16[1225,3072]{1,0:T(8,128)(2,1)}, f32[1225,3072]{1,0:T(8,128)}, f32[1225,3072]{1,0:T(8,128)}) fusion(f32[1225,3072]{1,0:T(8,128)S(1)} %fusion.135, f32[1225,16]{0,1:T(8,128)S(1)} %fusion.149, bf16[1,16,3072]{2,0,1:T(2,128)(2,1)S(1)} %fusion.64), kind=kOutput, calls=%fused_computation.9 | convolution fusion | flops 970905600 | bytes 52861504 | tf_op jit(solution)/shard_map/dot_general | solution.py:110
  1017.3 23.1 %add_convert_fusion = bf16[1225,3072]{1,0:T(8,128)(2,1)} fusion(f32[1225,3072]{1,0:T(8,128)} %get-tuple-element.32, f32[1225,3072]{1,0:T(8,128)} %fusion.137, f32[1225,3072]{1,0:T(8,128)} %get-tuple-element.51, f32[1225,16]{0,1:T(8,128)S(1)} %fusion.116, bf16[1,3072,16]{1,2,0:T(8,128)(2,1)S(1)} %copy.292), kind=kOutput, calls=%fused_computation.8 | convolution fusion | flops 778982400 | bytes 52861504 | tf_op jit(solution)/shard_map/dot_general | solution.py:117
  1045.8 8.7 fusion.138
  1062.8 26.9 %all_to_all.186 = bf16[1225,4,192]{0,2,1:T(8,128)(2,1)S(1)} all-to-all(bf16[1225,4,192]{0,2,1:T(8,128)(2,1)S(1)} %bitcast.307), channel_id=1, replica_groups=mesh['dp'=2,'row'=4,'col'=4] {'row'}, dimensions={1} | all-to-all | bytes 3763200 | tf_op jit(solution)/shard_map/all_to_all | solution.py:88
  1114.9 23.5 %all-to-all-done.8 = bf16[4,1225,192]{1,2,0:T(8,128)(2,1)S(1)} async-done(((bf16[4,1225,192]{1,2,0:T(8,128)(2,1)}), bf16[4,1225,192]{1,2,0:T(8,128)(2,1)S(1)}, u32[]{:S(2)}, u32[]{:S(2)}) %all-to-all-start.8) | async-done | bytes 1881632 | tf_op jit(solution)/shard_map/all_to_all | solution.py:94
  1154.1 9.9 fusion.136
  1171.0 7.5 all-to-all-done.9
  1187.7 9.3 reshape.212
  1197.0 11.3 convert_bitcast_fusion.5
  1208.2 21.7 %multiply_reduce_fusion = (f32[25,3,196]{2,1,0:T(4,128)S(1)}, f32[25,3,196,196]{2,3,1,0:T(8,128)}) fusion(f32[25,3,196,196]{2,3,1,0:T(8,128)} %get-tuple-element.50, f32[25,3,196]{2,1,0:T(4,128)S(1)} %log_add_fusion, bf16[25,196,3,1,64]{1,0,4,3,2:T(8,128)(2,1)} %get-tuple-element.35, bf16[25,196,3,64]{1,0,3,2:T(8,128)(2,1)S(1)} %reshape.212), kind=kOutput, calls=%fused_computation.2 | convolution fusion | flops 377422528 | bytes 26930400 | tf_op jit(solution)/shard_map/nqhc,nkhc->nhqk/dot_general | solution.py:185
  1230.0 11.2 multiply_convert_fusion
  1249.0 30.3 %copy.261 = f32[25,3,196,196]{0,3,2,1:T(8,128)} copy(bf16[25,3,196,196]{2,3,1,0:T(8,128)(2,1)} %copy-done.2) | data formatting | bytes 17287200 | tf_op jit(solution)/shard_map/reshape | solution.py:194
  1279.4 64.6 %reshape.221 = f32[25,3,14,14,14,14]{0,5,4,3,2,1:T(8,128)} reshape(f32[25,3,196,196]{0,3,2,1:T(8,128)} %copy.261) | data formatting | bytes 23049600 | tf_op jit(solution)/shard_map/reshape | solution.py:194
  1344.0 94.7 %fusion.128 = (f32[25,3,14,14,14]{0,4,3,2,1:T(8,128)}, f32[25,3,14,14,14]{0,4,3,2,1:T(8,128)}) fusion(f32[25,3,14,14,14,14]{0,5,4,3,2,1:T(8,128)} %reshape.221), kind=kLoop, calls=%fused_computation.231 | loop fusion | flops 5350800 | bytes 13171200 | tf_op jit(solution)/shard_map/reduce_sum | solution.py:195
  1438.7 10.2 fusion.14
  1449.0 7.8 bitcast_add_fusion
  1456.8 8.0 copy.264
  1464.8 8.9 reshape.215
  1473.7 8.4 copy.265
  1482.1 8.5 fusion.47
  1494.7 11.8 copy.269
  1506.5 24.2 %convert_element_type.249 = bf16[4,1225,576]{1,0,2:T(4,128)(2,1)} reshape(bf16[25,196,3,3,64]{1,0,4,3,2:T(8,128)(2,1)} %copy.269) | data formatting | bytes 11289600 | tf_op jit(solution)/shard_map/convert_element_type | solution.py:205
  1577.8 31.0 %all-to-all-done.10 = bf16[4,1225,576]{1,2,0:T(8,128)(2,1)} async-done(((bf16[4,1225,576]{1,2,0:T(8,128)(2,1)}), bf16[4,1225,576]{1,2,0:T(8,128)(2,1)}, u32[]{:S(2)}, u32[]{:S(2)}) %all-to-all-start.10) | async-done | bytes 5644832 | tf_op jit(solution)/shard_map/all_to_all | solution.py:94
  1612.6 7.4 fusion.140
  1634.6 7.3 fusion.142
  1643.2 17.6 all-to-all-done.11
  1678.7 10.9 all-reduce.2
  1689.7 9.7 fusion.37
  1699.4 106.6 %all-reduce.6.cloned.1.call-done = (f32[8,768,16]{1,2,0:T(8,128)}, f32[8,16,2304]{2,1,0:T(8,128)}, f32[8,768,16]{1,2,0:T(8,128)}, f32[8,16,768]{2,1,0:T(8,128)},...) async-done(((f32[8,768,16]{1,2,0:T(8,128)}, f32[8,16,2304]{2,1,0:T(8,128)}, f32[8,768,16]{1,2,0:T(8,128)}, ...) | async-done | bytes 6291472 | tf_op jit(solution)/shard_map/psum | solution.py:326
  (354 shorter events, 331.7 us)
Async XLA Ops:
  7.2 354.6 %copy-start = (bf16[27,64]{1,0:T(8,128)(2,1)S(1)}, bf16[27,64]{1,0:T(8,128)(2,1)}, u32[]{:S(2)}) copy-start(bf16[27,64]{1,0:T(8,128)(2,1)} %param.28) | copy-start | bytes 10372
  7.2 12.9 copy-start.90
  7.2 12.9 copy-start.4
  7.2 225.9 %all-gather.7.cloned.1.call-start = ((), (), s32[]{:S(2)}) async-start(), calls=%async_computation.12 | async-start | bytes 4423680 | tf_op jit(solution)/shard_map/all_gather | solution.py:250
  20.1 14.9 copy-start.86
  41.5 191.2 %all-to-all-start = ((bf16[4,1225,192]{1,2,0:T(8,128)(2,1)}), bf16[4,1225,192]{1,2,0:T(8,128)(2,1)S(1)}, u32[]{:S(2)}, u32[]{:S(2)}) async-start(bf16[4,1225,192]{1,2,0:T(8,128)(2,1)} %copy.222), calls=%async_computation | async-start | bytes 3932160 | tf_op jit(solution)/shard_map/all_to_all | solution.py:94
  45.1 119.6 %copy-start.76 = (bf16[8,192,16]{1,2,0:T(8,128)(2,1)S(1)}, bf16[8,192,16]{1,2,0:T(8,128)(2,1)}, u32[]{:S(2)}) copy-start(bf16[8,192,16]{1,2,0:T(8,128)(2,1)} %param.34) | copy-start | bytes 147460
  45.1 317.2 %all-gather.15.cloned.1.call-start = ((), (), s32[]{:S(2)}) async-start(), calls=%async_computation.16 | async-start | bytes 1474560 | tf_op jit(solution)/shard_map/all_gather | solution.py:269
  45.9 119.1 %copy-start.77 = (bf16[8,192,16]{1,2,0:T(8,128)(2,1)S(1)}, bf16[8,192,16]{1,2,0:T(8,128)(2,1)}, u32[]{:S(2)}) copy-start(bf16[8,192,16]{1,2,0:T(8,128)(2,1)} %param.32) | copy-start | bytes 147460
  45.9 120.1 %copy-start.78 = (bf16[8,192,16]{1,2,0:T(8,128)(2,1)S(1)}, bf16[8,192,16]{1,2,0:T(8,128)(2,1)}, u32[]{:S(2)}) copy-start(bf16[8,192,16]{1,2,0:T(8,128)(2,1)} %param.30) | copy-start | bytes 147460
  171.6 56.4 %copy-start.91 = (s32[8,1]{0,1:T(1,128)S(1)}, s32[8,1]{0,1:T(1,128)}, u32[]{:S(2)}) copy-start(s32[8,1]{0,1:T(1,128)} %param.21) | copy-start | bytes 100
  228.7 11.7 copy-start.51
  256.5 81.9 %copy-start.79 = (bf16[8,16,192]{2,1,0:T(8,128)(2,1)S(1)}, bf16[8,16,192]{2,1,0:T(8,128)(2,1)}, u32[]{:S(2)}) copy-start(bf16[8,16,192]{2,1,0:T(8,128)(2,1)} %param.33) | copy-start | bytes 147460
  256.5 105.8 %all-to-all-start.1 = ((bf16[1225,4,576]{0,2,1:T(8,128)(2,1)}), bf16[1225,4,576]{0,2,1:T(8,128)(2,1)}, u32[]{:S(2)}, u32[]{:S(2)}) async-start(bf16[1225,4,576]{0,2,1:T(8,128)(2,1)} %bitcast.293), calls=%async_computation.1 | async-start | bytes 11796480 | tf_op jit(solution)/shard_map/all_to_all | solution.py:98
  261.8 91.5 %copy-start.93 = (u32[32]{0:T(128)S(1)}, u32[32]{0:T(128)}, u32[]{:S(2)}) copy-start(u32[32]{0:T(128)} %constant.173) | copy-start | bytes 388
  261.8 92.7 %copy-start.92 = (bf16[192]{0:T(256)(128)(2,1)S(1)}, bf16[192]{0:T(256)(128)(2,1)}, u32[]{:S(2)}) copy-start(bf16[192]{0:T(256)(128)(2,1)} %param.23) | copy-start | bytes 1156
  261.8 100.2 %copy-start.89 = (bf16[27,64]{1,0:T(8,128)(2,1)S(1)}, bf16[27,64]{1,0:T(8,128)(2,1)}, u32[]{:S(2)}) copy-start(bf16[27,64]{1,0:T(8,128)(2,1)} %param.29) | copy-start | bytes 10372
  261.9 572.0 %all-gather.11.cloned.1.call-start = ((), (), s32[]{:S(2)}) async-start(), calls=%async_computation.14 | async-start | bytes 1474560 | tf_op jit(solution)/shard_map/all_gather | solution.py:268
  262.6 571.3 %all-gather.9.cloned.1.call-start = ((), (), s32[]{:S(2)}) async-start(), calls=%async_computation.13 | async-start | bytes 1474560 | tf_op jit(solution)/shard_map/all_gather | solution.py:251
  338.4 590.4 %all-gather.17.cloned.1.call-start = ((), (), s32[]{:S(2)}) async-start(), calls=%async_computation.17 | async-start | bytes 5898240 | tf_op jit(solution)/shard_map/all_gather | solution.py:276
  362.0 190.1 %copy-start.63 = (bf16[14,14,64,1,1]{2,1,4,3,0:T(8,128)(2,1)}, bf16[14,14,64,1,1]{2,1,4,3,0:T(8,128)(2,1)S(1)}, u32[]{:S(2)}) copy-start(bf16[14,14,64,1,1]{2,1,4,3,0:T(8,128)(2,1)S(1)} %fusion.61) | copy-start | bytes 75268
  362.2 55.7 %copy-start.65 = (bf16[14,14,64]{2,1,0:T(8,128)(2,1)}, bf16[14,14,64]{2,1,0:T(8,128)(2,1)S(1)}, u32[]{:S(2)}) copy-start(bf16[14,14,64]{2,1,0:T(8,128)(2,1)S(1)} %convolution_convert_fusion) | copy-start | bytes 75268
  405.0 13.0 copy-start.8
  650.8 39.1 %copy-start.9 = (bf16[25,196,3,1,64]{1,0,4,3,2:T(8,128)(2,1)S(1)}, bf16[25,196,3,1,64]{1,0,4,3,2:T(8,128)(2,1)}, u32[]{:S(2)}) copy-start(bf16[25,196,3,1,64]{1,0,4,3,2:T(8,128)(2,1)} %copy-done.8) | copy-start | bytes 5644804
  714.4 9.8 copy-start.35
  714.4 9.8 copy-start.23
  724.2 10.2 copy-start.53
  746.5 27.9 %all-to-all-start.2 = ((bf16[4,1225,192]{1,2,0:T(8,128)(2,1)}), bf16[4,1225,192]{1,2,0:T(8,128)(2,1)S(1)}, u32[]{:S(2)}, u32[]{:S(2)}) async-start(bf16[4,1225,192]{1,2,0:T(8,128)(2,1)} %copy.240), calls=%async_computation.2 | async-start | bytes 3932160 | tf_op jit(solution)/shard_map/all_to_all | solution.py:94
  753.2 8.8 copy-start.80
  753.2 9.8 copy-start.41
  753.2 9.8 copy-start.85
  775.7 70.0 %all-to-all-start.6 = ((bf16[4,1225,192]{1,2,0:T(8,128)(2,1)}), bf16[4,1225,192]{1,2,0:T(8,128)(2,1)S(1)}, u32[]{:S(2)}, u32[]{:S(2)}) async-start(bf16[4,1225,192]{1,2,0:T(8,128)(2,1)} %copy.253), calls=%async_computation.6 | async-start | bytes 3932160 | tf_op jit(solution)/shard_map/all_to_all | solution.py:82
  779.3 188.6 %all-gather.13.cloned.1.call-start = ((), (), s32[]{:S(2)}) async-start(), calls=%async_computation.15 | async-start | bytes 5898240 | tf_op jit(solution)/shard_map/all_gather | solution.py:275
  845.7 53.3 %copy-start.11 = (bf16[4,1225,192]{1,2,0:T(8,128)(2,1)}, bf16[4,1225,192]{1,2,0:T(8,128)(2,1)S(1)}, u32[]{:S(2)}) copy-start(bf16[4,1225,192]{1,2,0:T(8,128)(2,1)S(1)} %all-to-all-done.6) | copy-start | bytes 5644804
  845.7 53.6 %all-to-all-start.3 = ((bf16[1225,4,192]{0,2,1:T(8,128)(2,1)}), bf16[1225,4,192]{0,2,1:T(8,128)(2,1)}, u32[]{:S(2)}, u32[]{:S(2)}) async-start(bf16[1225,4,192]{0,2,1:T(8,128)(2,1)} %bitcast.305), calls=%async_computation.3 | async-start | bytes 3932160 | tf_op jit(solution)/shard_map/all_to_all | solution.py:102
  858.0 9.8 copy-start.42
  858.0 10.0 copy-start.72
  867.8 149.5 %copy-start.55 = (bf16[1,3072,16]{1,2,0:T(8,128)(2,1)}, bf16[1,3072,16]{1,2,0:T(8,128)(2,1)S(1)}, u32[]{:S(2)}) copy-start(bf16[1,3072,16]{1,2,0:T(8,128)(2,1)S(1)} %copy.292) | copy-start | bytes 294916
  868.1 30.9 %copy-start.69 = (bf16[1,16,768]{2,0,1:T(2,128)(2,1)}, bf16[1,16,768]{2,0,1:T(2,128)(2,1)S(1)}, u32[]{:S(2)}) copy-start(bf16[1,16,768]{2,0,1:T(2,128)(2,1)S(1)} %fusion.119) | copy-start | bytes 73732
  899.3 118.0 %copy-start.61 = (f32[1225,16]{0,1:T(8,128)}, f32[1225,16]{0,1:T(8,128)S(1)}, u32[]{:S(2)}) copy-start(f32[1225,16]{0,1:T(8,128)S(1)} %fusion.116) | copy-start | bytes 235204
  924.1 29.0 %all-to-all-start.4 = ((bf16[4,1225,192]{1,2,0:T(8,128)(2,1)}), bf16[4,1225,192]{1,2,0:T(8,128)(2,1)}, u32[]{:S(2)}, u32[]{:S(2)}) async-start(bf16[4,1225,192]{1,2,0:T(8,128)(2,1)} %copy.247), calls=%async_computation.4 | async-start | bytes 3932160 | tf_op jit(solution)/shard_map/all_to_all | solution.py:82
  1045.7 8.7 copy-start.37
  1045.8 8.7 copy-start.7
  1109.1 29.3 %copy-start.68 = (bf16[1,16,768]{2,0,1:T(2,128)(2,1)S(1)}, bf16[1,16,768]{2,0,1:T(2,128)(2,1)}, u32[]{:S(2)}) copy-start(bf16[1,16,768]{2,0,1:T(2,128)(2,1)} %fusion.123) | copy-start | bytes 73732
  1110.5 27.9 %all-to-all-start.8 = ((bf16[4,1225,192]{1,2,0:T(8,128)(2,1)}), bf16[4,1225,192]{1,2,0:T(8,128)(2,1)S(1)}, u32[]{:S(2)}, u32[]{:S(2)}) async-start(bf16[4,1225,192]{1,2,0:T(8,128)(2,1)} %copy.256), calls=%async_computation.8 | async-start | bytes 3932160 | tf_op jit(solution)/shard_map/all_to_all | solution.py:94
  1149.2 14.9 slice-start
  1149.2 29.3 %all-to-all-start.9 = ((bf16[1225,4,192]{0,2,1:T(8,128)(2,1)}), bf16[1225,4,192]{0,2,1:T(8,128)(2,1)}, u32[]{:S(2)}, u32[]{:S(2)}) async-start(bf16[1225,4,192]{0,2,1:T(8,128)(2,1)} %bitcast.306), calls=%async_computation.9 | async-start | bytes 3932160 | tf_op jit(solution)/shard_map/all_to_all | solution.py:98
  1154.1 10.0 slice-start.1
  1154.1 10.0 copy-start.56
  1178.5 358.2 %all-to-all-start.5 = ((bf16[1225,4,192]{0,2,1:T(8,128)(2,1)}), bf16[1225,4,192]{0,2,1:T(8,128)(2,1)}, u32[]{:S(2)}, u32[]{:S(2)}) async-start(bf16[1225,4,192]{0,2,1:T(8,128)(2,1)} %bitcast.38), calls=%async_computation.5 | async-start | bytes 3932160 | tf_op jit(solution)/shard_map/all_to_all | solution.py:88
  1230.0 14.2 copy-start.10
  1343.9 94.8 %copy-start.66 = (bf16[14,14,64]{2,1,0:T(8,128)(2,1)S(1)}, bf16[14,14,64]{2,1,0:T(8,128)(2,1)}, u32[]{:S(2)}) copy-start(bf16[14,14,64]{2,1,0:T(8,128)(2,1)} %copy-done.65) | copy-start | bytes 75268
  1438.7 10.3 copy-start.14
  1438.7 10.3 copy-start.64
  1536.7 8.7 copy-start.40
  1536.7 17.4 slice-start.2
  1536.7 72.1 %all-to-all-start.10 = ((bf16[4,1225,576]{1,2,0:T(8,128)(2,1)}), bf16[4,1225,576]{1,2,0:T(8,128)(2,1)}, u32[]{:S(2)}, u32[]{:S(2)}) async-start(bf16[4,1225,576]{1,2,0:T(8,128)(2,1)} %copy.270), calls=%async_computation.10 | async-start | bytes 11796480 | tf_op jit(solution)/shard_map/all_to_all | solution.py:94
  1566.1 10.0 copy-start.19
  1566.1 10.0 copy-start.48
  1571.9 37.0 %copy-start.52 = (bf16[1,16,2304]{2,0,1:T(2,128)(2,1)S(1)}, bf16[1,16,2304]{2,0,1:T(2,128)(2,1)}, u32[]{:S(2)}) copy-start(bf16[1,16,2304]{2,0,1:T(2,128)(2,1)} %copy-done.51) | copy-start | bytes 221188
  1623.1 8.8 copy-start.16
  1627.2 33.6 %all-to-all-start.11 = ((bf16[1225,4,192]{0,2,1:T(8,128)(2,1)}), bf16[1225,4,192]{0,2,1:T(8,128)(2,1)}, u32[]{:S(2)}, u32[]{:S(2)}) async-start(bf16[1225,4,192]{0,2,1:T(8,128)(2,1)} %bitcast.304), calls=%async_computation.11 | async-start | bytes 3932160 | tf_op jit(solution)/shard_map/all_to_all | solution.py:102
  1631.8 174.2 %all-reduce.6.cloned.1.call-start = ((), (), s32[]{:S(2)}) async-start(), calls=%async_computation.18 | async-start | bytes 12582912 | tf_op jit(solution)/shard_map/psum | solution.py:326
  1689.6 130.2 %copy-start.1 = (bf16[27,64]{1,0:T(8,128)(2,1)S(1)}, bf16[27,64]{1,0:T(8,128)(2,1)}, u32[]{:S(2)}) copy-start(bf16[27,64]{1,0:T(8,128)(2,1)} %param.28) | copy-start | bytes 10372
  (52 other events, 277.8 us)
Sparse Core Ops, SparseCore 0:
  20.2 108.6 all-gather.6
  130.5 16.0 all-gather.14
  264.3 24.6 all-gather.10
  338.5 29.8 all-gather.8
  369.8 88.5 all-gather.16
  834.0 100.3 all-gather.12
  1643.3 162.6 all-reduce.5
where the time goes:
time: 1840 us; the launch traced here: 1830 us
  local copies, waits for them, and re-layouts  647 us (35%)
  blocking collectives  412 us (22%)
  matrix products  314 us (17%)
  waiting for transfers between devices  211 us (11%)
  other arithmetic  177 us (10%)
  starting transfers between devices  49.4 us (3%)
    add x6, local copies, waits for them, and re-layouts, score_matrix(): shaped + rel_rows[:, :, :, :, :, None] + rel_cols[:, :, :, :, None, :]  251 us
    all_gather x1, blocking collectives, body(): lax.all_gather(qkv_up, 'col', axis=2, tiled=True)  118 us
    psum x1, waiting for transfers between devices, body(): lax.psum((spread_pick(own_pick, qkv_pair[0]), spread_pick(own_pick, qkv_p...  107 us
    reshape x2, local copies, waits for them, and re-layouts, attend_back(): grad_s.astype(jnp.float32).reshape(windows, heads_local, WIN, WIN, WIN, WIN)  94.9 us
    reduce_sum x1, other arithmetic, attend_back(): along_rows = jnp.sum(split_grad, axis=5)  94.7 us
    all_gather x1, blocking collectives, body(): lax.all_gather(proj_weight, 'row', axis=1, tiled=True)  74.5 us
    all_to_all x4, waiting for transfers between devices, token_rows(): lax.all_to_all(values, 'row', split_axis=0, concat_axis=1, tiled=True)  65.1 us
    dot_general x4, matrix products, adapted_local(): jnp.dot(reduced, up_mat.astype(jnp.float32), precision=PRECISE)  53.4 us
  transfers between devices with their start and end apart: 18, of which 7 were waited for; matrix products, arithmetic and copies ran while one was open for 52% of the time, Pallas kernels for 0%

commit v1 on v0

--- a/solution.py
+++ b/solution.py
@@ -12,6 +12,18 @@
 IMG_TOK = 4900
 PRECISE = lax.Precision.HIGHEST
 EPSILON = 1e-06
+
+
+def doubled_up(array, axis, dim):
+    ways, here = (lax.axis_size(axis), lax.axis_index(axis))
+    grown, reach = (array, 1)
+    while reach < ways:
+        theirs = lax.ppermute(grown, axis, [(d, d ^ reach) for d in range(ways)])
+        mine_first = jnp.concatenate([grown, theirs], axis=dim)
+        theirs_first = jnp.concatenate([theirs, grown], axis=dim)
+        grown = jnp.where(here & reach == 0, mine_first, theirs_first)
+        reach = 2 * reach
+    return grown
 
 
 def exact_gelu(values):
@@ -249,7 +261,7 @@
     qkv_full, proj_full, qkv_up_all, proj_dn_all = (
         lax.all_gather(qkv_part, "col", axis=1, tiled=True),
         lax.all_gather(proj_part, "col", axis=0, tiled=True),
-        lax.all_gather(qkv_up, "col", axis=2, tiled=True),
+        doubled_up(qkv_up, "col", 2),
         lax.all_gather(proj_down, "col", axis=1, tiled=True),
     )
     qkv_dn = pick_one(qkv_dn_part, own_pick)

time: 1840 us -> 1770 us (0.962)
  blocking collectives: 412 us -> 324 us
    all_gather x1 -> x0, blocking collectives: 118 us -> none  [body(): lax.all_gather(qkv_up, 'col', axis=2, tiled=True)]
  transfers between devices with their start and end apart: 18 -> 20, of which waited for: 7 -> 8; matrix products, arithmetic and copies ran while one was open for 52% -> 55% of each run, Pallas kernels for 0% -> 0%
where the time goes in v1:
time: 1770 us; the launch traced here: 1750 us
  local copies, waits for them, and re-layouts  644 us (36%)
  blocking collectives  324 us (18%)
  matrix products  315 us (18%)
  waiting for transfers between devices  218 us (12%)
  other arithmetic  180 us (10%)
  starting transfers between devices  52.8 us (3%)
    add x6, local copies, waits for them, and re-layouts, score_matrix(): shaped + rel_rows[:, :, :, :, :, None] + rel_cols[:, :, :, :, None, :]  251 us
    psum x1, waiting for transfers between devices, body(): lax.psum((spread_pick(own_pick, qkv_pair[0]), spread_pick(own_pick, qkv_p...  107 us
    reshape x2, local copies, waits for them, and re-layouts, attend_back(): grad_s.astype(jnp.float32).reshape(windows, heads_local, WIN, WIN, WIN, WIN)  95.1 us
    reduce_sum x1, other arithmetic, attend_back(): along_rows = jnp.sum(split_grad, axis=5)  94.8 us
    all_gather x1, blocking collectives, body(): lax.all_gather(proj_weight, 'row', axis=1, tiled=True)  74.7 us
    all_to_all x4, waiting for transfers between devices, token_rows(): lax.all_to_all(values, 'row', split_axis=0, concat_axis=1, tiled=True)  65.1 us
    dot_general x4, matrix products, adapted_local(): jnp.dot(reduced, up_mat.astype(jnp.float32), precision=PRECISE)  53.5 us
    all_gather x1, blocking collectives, body(): lax.all_gather(proj_down, 'col', axis=1, tiled=True)  38.3 us
  transfers between devices with their start and end apart: 20, of which 8 were waited for; matrix products, arithmetic and copies ran while one was open for 55% of the time, Pallas kernels for 0%

profile of v1, /device:TPU:0, one launch (start us, length us, event | category | flops | bytes accessed | tf_op | source)
XLA Modules:
  0.0 1750.4 jit_solution(10698132049476670270)
XLA Ops:
  7.3 11.5 all_gather.48
  20.9 11.5 all-reduce.3
  47.9 30.9 %all_gather.58 = bf16[8,768,16]{2,0,1:T(8,128)(2,1)S(1)} all-gather(bf16[8,192,16]{2,0,1:T(8,128)(2,1)} %copy.246), channel_id=1, replica_groups=mesh['dp'=2,'row'=4,'col'=4] {'row'}, dimensions={1}, use_global_device_ids=true | all-gather | bytes 245760 | tf_op jit(solution)/shard_map/all_gather | solution.py:282
  80.8 38.3 %all_gather.53 = bf16[8,768,16]{2,0,1:T(8,128)(2,1)} all-gather(bf16[8,192,16]{2,0,1:T(8,128)(2,1)} %copy.240), channel_id=1, replica_groups=mesh['dp'=2,'row'=4,'col'=4] {'col'}, dimensions={1}, use_global_device_ids=true | all-gather | bytes 245760 | tf_op jit(solution)/shard_map/all_gather | solution.py:265
  120.9 17.0 all_gather.50
  146.9 7.8 collective-permute-done.1
  156.7 7.0 fusion.134
  163.7 7.2 fusion.8
  170.9 9.4 copy.223
  186.5 74.7 %all_gather.51 = bf16[192,768]{0,1:T(8,128)(2,1)S(1)} all-gather(bf16[192,192]{0,1:T(8,128)(2,1)S(1)} %copy.238), channel_id=1, replica_groups=mesh['dp'=2,'row'=4,'col'=4] {'row'}, dimensions={1}, use_global_device_ids=true | all-gather | bytes 368640 | tf_op jit(solution)/shard_map/all_gather | solution.py:257
  262.5 13.0 all_gather.54
  286.1 9.7 copy.224
  295.8 26.8 %reshape.211 = bf16[25,196,3,3,64]{1,0,4,3,2:T(8,128)(2,1)} reshape(bf16[4,1225,576]{1,0,2:T(4,128)(2,1)} %copy.224) | data formatting | bytes 11289600 | tf_op jit(solution)/shard_map/reshape | solution.py:154
  334.3 7.3 reshape_squeeze.4
  341.6 8.6 fusion.52
  350.7 21.4 %add.271 = f32[25,3,14,14,14,14]{0,5,4,3,2,1:T(8,128)} broadcast(f32[25,3,14,14,14]{0,4,3,2,1:T(8,128)S(1)} %copy.233), dimensions={0,1,2,3,5} | broadcast | bytes 12348000 | tf_op jit(solution)/shard_map/add | solution.py:172
  372.1 64.5 %add.272 = f32[25,3,196,196]{0,3,2,1:T(8,128)} reshape(f32[25,3,14,14,14,14]{0,5,4,3,2,1:T(8,128)} %add.271) | data formatting | bytes 23049600 | tf_op jit(solution)/shard_map/add | solution.py:172
  436.6 39.1 %copy.234 = f32[25,3,196,196]{2,3,1,0:T(8,128)} copy(f32[25,3,196,196]{0,3,2,1:T(8,128)} %add.272) | data formatting | bytes 23049600 | tf_op jit(solution)/shard_map/add | solution.py:172
  475.7 8.6 fusion.49
  487.0 22.8 %add.268 = f32[25,3,14,14,14,14]{0,5,4,3,2,1:T(8,128)} broadcast(f32[25,3,14,14,14]{0,4,3,2,1:T(8,128)} %copy.230), dimensions={0,1,2,3,4} | broadcast | bytes 12348000 | tf_op jit(solution)/shard_map/add | solution.py:172
  509.8 64.5 %add.269 = f32[25,3,196,196]{0,3,2,1:T(8,128)} reshape(f32[25,3,14,14,14,14]{0,5,4,3,2,1:T(8,128)} %add.268) | data formatting | bytes 23049600 | tf_op jit(solution)/shard_map/add | solution.py:172
  574.3 39.1 %copy.231 = f32[25,3,196,196]{2,3,1,0:T(8,128)} copy(f32[25,3,196,196]{0,3,2,1:T(8,128)} %add.269) | data formatting | bytes 23049600 | tf_op jit(solution)/shard_map/add | solution.py:172
  613.4 24.8 %fusion.133 = (f32[25,3,196]{2,1,0:T(4,128)S(1)}, f32[25,3,196,196]{2,3,1,0:T(8,128)}) fusion(f32[25,3,196,196]{2,3,1,0:T(8,128)} %copy.234, f32[25,3,196,196]{2,3,1,0:T(8,128)} %copy.231, bf16[25,196,3,1,64]{1,0,4,3,2:T(8,128)(2,1)} %get-tuple-element.37, bf16[25,196,3,1,64]{1,0,4,3,2:T(8,128)(2,1)S(1)} %copy-done.9), kind=kOutput, calls=%fused_computation.237 | convolution fusion | flops 380303744 | bytes 38396400 | tf_op jit(solution)/shard_map/nqhc,nkhc->nhqk/dot_general | solution.py:161
  638.2 9.8 fusion.6
  648.0 10.1 convert_bitcast_fusion.6
  659.7 7.3 convert_element_type.214
  687.3 10.6 all-to-all-done.2
  702.8 33.6 %all_gather.63 = bf16[8,16,768]{1,0,2:T(8,128)(2,1)S(1)} all-gather(bf16[8,16,192]{1,0,2:T(8,128)(2,1)} %copy.247), channel_id=1, replica_groups=mesh['dp'=2,'row'=4,'col'=4] {'row'}, dimensions={2}, use_global_device_ids=true | all-gather | bytes 245760 | tf_op jit(solution)/shard_map/all_gather | solution.py:283
  738.0 19.2 %all_gather.62 = bf16[8,3072,16]{1,2,0:T(8,128)(2,1)S(1)} all-gather(bf16[8,768,16]{1,2,0:T(8,128)(2,1)} %param.36), channel_id=1, replica_groups=mesh['dp'=2,'row'=4,'col'=4] {'col'}, dimensions={1}, use_global_device_ids=true | all-gather | bytes 983040 | tf_op jit(solution)/shard_map/all_gather | solution.py:290
  773.7 7.8 fusion.62
  781.5 9.8 copy.289
  791.5 30.2 %all_gather.59 = bf16[8,16,3072]{2,1,0:T(8,128)(2,1)S(1)} all-gather(bf16[8,16,768]{2,1,0:T(8,128)(2,1)S(1)} %copy-done.71), channel_id=1, replica_groups=mesh['dp'=2,'row'=4,'col'=4] {'col'}, dimensions={2}, use_global_device_ids=true | all-gather | bytes 983040 | tf_op jit(solution)/shard_map/all_gather | solution.py:289
  852.4 11.9 fusion.138
  864.3 12.4 all-to-all-done.4
  891.5 8.0 fusion.136
  899.5 41.5 %multiply_convert_fusion.1 = (bf16[1225,3072]{1,0:T(8,128)(2,1)}, f32[1225,3072]{1,0:T(8,128)}, f32[1225,3072]{1,0:T(8,128)}) fusion(f32[1225,3072]{1,0:T(8,128)S(1)} %fusion.136, f32[1225,16]{0,1:T(8,128)S(1)} %fusion.150, bf16[1,16,3072]{2,0,1:T(2,128)(2,1)S(1)} %fusion.64), kind=kOutput, calls=%fused_computation.9 | convolution fusion | flops 970905600 | bytes 52861504 | tf_op jit(solution)/shard_map/dot_general | solution.py:122
  941.0 22.8 %add_convert_fusion = bf16[1225,3072]{1,0:T(8,128)(2,1)} fusion(f32[1225,3072]{1,0:T(8,128)} %get-tuple-element.32, f32[1225,3072]{1,0:T(8,128)} %fusion.138, f32[1225,3072]{1,0:T(8,128)} %get-tuple-element.51, f32[1225,16]{0,1:T(8,128)S(1)} %fusion.118, bf16[1,3072,16]{1,2,0:T(8,128)(2,1)S(1)} %copy.289), kind=kOutput, calls=%fused_computation.8 | convolution fusion | flops 778982400 | bytes 52861504 | tf_op jit(solution)/shard_map/dot_general | solution.py:129
  969.2 8.7 fusion.139
  986.2 27.0 %all_to_all.186 = bf16[1225,4,192]{0,2,1:T(8,128)(2,1)S(1)} all-to-all(bf16[1225,4,192]{0,2,1:T(8,128)(2,1)S(1)} %bitcast.306), channel_id=1, replica_groups=mesh['dp'=2,'row'=4,'col'=4] {'row'}, dimensions={1} | all-to-all | bytes 3763200 | tf_op jit(solution)/shard_map/all_to_all | solution.py:100
  1038.4 23.5 %all-to-all-done.8 = bf16[4,1225,192]{1,2,0:T(8,128)(2,1)S(1)} async-done(((bf16[4,1225,192]{1,2,0:T(8,128)(2,1)}), bf16[4,1225,192]{1,2,0:T(8,128)(2,1)S(1)}, u32[]{:S(2)}, u32[]{:S(2)}) %all-to-all-start.8) | async-done | bytes 1881632 | tf_op jit(solution)/shard_map/all_to_all | solution.py:106
  1077.7 9.9 fusion.137
  1094.5 7.5 all-to-all-done.9
  1111.0 9.3 reshape.212
  1120.3 11.2 convert_bitcast_fusion.5
  1131.6 21.7 %multiply_reduce_fusion = (f32[25,3,196]{2,1,0:T(4,128)S(1)}, f32[25,3,196,196]{2,3,1,0:T(8,128)}) fusion(f32[25,3,196,196]{2,3,1,0:T(8,128)} %get-tuple-element.50, f32[25,3,196]{2,1,0:T(4,128)S(1)} %log_add_fusion, bf16[25,196,3,1,64]{1,0,4,3,2:T(8,128)(2,1)} %get-tuple-element.35, bf16[25,196,3,64]{1,0,3,2:T(8,128)(2,1)S(1)} %reshape.212), kind=kOutput, calls=%fused_computation.2 | convolution fusion | flops 377422528 | bytes 26930400 | tf_op jit(solution)/shard_map/nqhc,nkhc->nhqk/dot_general | solution.py:197
  1153.3 11.2 multiply_convert_fusion
  1172.4 30.4 %copy.258 = f32[25,3,196,196]{0,3,2,1:T(8,128)} copy(bf16[25,3,196,196]{2,3,1,0:T(8,128)(2,1)} %copy-done.2) | data formatting | bytes 17287200 | tf_op jit(solution)/shard_map/reshape | solution.py:206
  1202.8 64.7 %reshape.221 = f32[25,3,14,14,14,14]{0,5,4,3,2,1:T(8,128)} reshape(f32[25,3,196,196]{0,3,2,1:T(8,128)} %copy.258) | data formatting | bytes 23049600 | tf_op jit(solution)/shard_map/reshape | solution.py:206
  1267.6 94.8 %fusion.129 = (f32[25,3,14,14,14]{0,4,3,2,1:T(8,128)}, f32[25,3,14,14,14]{0,4,3,2,1:T(8,128)}) fusion(f32[25,3,14,14,14,14]{0,5,4,3,2,1:T(8,128)} %reshape.221), kind=kLoop, calls=%fused_computation.234 | loop fusion | flops 5350800 | bytes 13171200 | tf_op jit(solution)/shard_map/reduce_sum | solution.py:207
  1362.3 10.0 fusion.14
  1372.4 7.8 bitcast_add_fusion
  1380.2 8.2 copy.261
  1388.4 8.9 reshape.215
  1397.4 8.4 copy.262
  1405.8 8.5 fusion.47
  1418.3 11.8 copy.266
  1430.2 24.2 %convert_element_type.249 = bf16[4,1225,576]{1,0,2:T(4,128)(2,1)} reshape(bf16[25,196,3,3,64]{1,0,4,3,2:T(8,128)(2,1)} %copy.266) | data formatting | bytes 11289600 | tf_op jit(solution)/shard_map/convert_element_type | solution.py:217
  1501.4 31.0 %all-to-all-done.10 = bf16[4,1225,576]{1,2,0:T(8,128)(2,1)} async-done(((bf16[4,1225,576]{1,2,0:T(8,128)(2,1)}), bf16[4,1225,576]{1,2,0:T(8,128)(2,1)}, u32[]{:S(2)}, u32[]{:S(2)}) %all-to-all-start.10) | async-done | bytes 5644832 | tf_op jit(solution)/shard_map/all_to_all | solution.py:106
  1536.2 7.2 fusion.141
  1558.1 7.3 fusion.143
  1566.6 17.6 %all-to-all-done.11 = bf16[1225,4,192]{0,2,1:T(8,128)(2,1)} async-done(((bf16[1225,4,192]{0,2,1:T(8,128)(2,1)}), bf16[1225,4,192]{0,2,1:T(8,128)(2,1)}, u32[]{:S(2)}, u32[]{:S(2)}) %all-to-all-start.11) | async-done | bytes 1881632 | tf_op jit(solution)/shard_map/all_to_all | solution.py:114
  1602.2 10.9 all-reduce.2
  1613.2 9.7 fusion.37
  1622.9 106.5 %all-reduce.6.cloned.1.call-done = (f32[8,768,16]{1,2,0:T(8,128)}, f32[8,16,2304]{2,1,0:T(8,128)}, f32[8,768,16]{1,2,0:T(8,128)}, f32[8,16,768]{2,1,0:T(8,128)},...) async-done(((f32[8,768,16]{1,2,0:T(8,128)}, f32[8,16,2304]{2,1,0:T(8,128)}, f32[8,768,16]{1,2,0:T(8,128)}, ...) | async-done | bytes 6291472 | tf_op jit(solution)/shard_map/psum | solution.py:338
  (349 shorter events, 335.6 us)
Async XLA Ops:
  7.2 278.4 %copy-start = (bf16[27,64]{1,0:T(8,128)(2,1)S(1)}, bf16[27,64]{1,0:T(8,128)(2,1)}, u32[]{:S(2)}) copy-start(bf16[27,64]{1,0:T(8,128)(2,1)} %param.28) | copy-start | bytes 10372
  7.2 12.9 copy-start.86
  7.2 12.9 copy-start.4
  7.2 149.5 %all-gather.7.cloned.1.call-start = ((), (), s32[]{:S(2)}) async-start(), calls=%async_computation.12 | async-start | bytes 4423680 | tf_op jit(solution)/shard_map/all_gather | solution.py:262
  20.1 14.9 copy-start.82
  41.5 37.4 %copy-start.87 = (s32[8,1]{0,1:T(1,128)S(1)}, s32[8,1]{0,1:T(1,128)}, u32[]{:S(2)}) copy-start(s32[8,1]{0,1:T(1,128)} %param.21) | copy-start | bytes 100
  41.5 113.7 %all-to-all-start = ((bf16[4,1225,192]{1,2,0:T(8,128)(2,1)}), bf16[4,1225,192]{1,2,0:T(8,128)(2,1)S(1)}, u32[]{:S(2)}, u32[]{:S(2)}) async-start(bf16[4,1225,192]{1,2,0:T(8,128)(2,1)} %copy.220), calls=%async_computation | async-start | bytes 3932160 | tf_op jit(solution)/shard_map/all_to_all | solution.py:106
  45.2 240.8 %all-gather.15.cloned.1.call-start = ((), (), s32[]{:S(2)}) async-start(), calls=%async_computation.16 | async-start | bytes 1474560 | tf_op jit(solution)/shard_map/all_gather | solution.py:281
  45.2 92.6 %collective-permute-start = (bf16[8,16,576]{2,1,0:T(8,128)(2,1)}, bf16[8,16,576]{2,1,0:T(8,128)(2,1)}, u32[]{:S(2)}, u32[]{:S(2)}) collective-permute-start(bf16[8,16,576]{2,1,0:T(8,128)(2,1)} %param.31), channel_id=1, source_target_pairs={{0,1},{1,0},{2,3},{3,2},{4,5},{5,4},{6,7},{7,6},{8,9},{9,8},{10,11... | collective-permute-start | bytes 442376 | tf_op jit(solution)/shard_map/ppermute | solution.py:21
  137.8 16.9 copy-start.78
  137.9 16.9 copy-start.80
  139.2 15.4 collective-permute-start.1
  180.3 81.9 %copy-start.75 = (bf16[8,16,192]{2,1,0:T(8,128)(2,1)S(1)}, bf16[8,16,192]{2,1,0:T(8,128)(2,1)}, u32[]{:S(2)}) copy-start(bf16[8,16,192]{2,1,0:T(8,128)(2,1)} %param.33) | copy-start | bytes 147460
  180.3 105.8 %all-to-all-start.1 = ((bf16[1225,4,576]{0,2,1:T(8,128)(2,1)}), bf16[1225,4,576]{0,2,1:T(8,128)(2,1)}, u32[]{:S(2)}, u32[]{:S(2)}) async-start(bf16[1225,4,576]{0,2,1:T(8,128)(2,1)} %bitcast.292), calls=%async_computation.1 | async-start | bytes 11796480 | tf_op jit(solution)/shard_map/all_to_all | solution.py:110
  185.6 91.5 %copy-start.89 = (u32[32]{0:T(128)S(1)}, u32[32]{0:T(128)}, u32[]{:S(2)}) copy-start(u32[32]{0:T(128)} %constant.176) | copy-start | bytes 388
  185.6 92.7 %copy-start.88 = (bf16[192]{0:T(256)(128)(2,1)S(1)}, bf16[192]{0:T(256)(128)(2,1)}, u32[]{:S(2)}) copy-start(bf16[192]{0:T(256)(128)(2,1)} %param.23) | copy-start | bytes 1156
  185.6 100.2 %copy-start.85 = (bf16[27,64]{1,0:T(8,128)(2,1)S(1)}, bf16[27,64]{1,0:T(8,128)(2,1)}, u32[]{:S(2)}) copy-start(bf16[27,64]{1,0:T(8,128)(2,1)} %param.29) | copy-start | bytes 10372
  185.6 571.6 %all-gather.11.cloned.1.call-start = ((), (), s32[]{:S(2)}) async-start(), calls=%async_computation.14 | async-start | bytes 1474560 | tf_op jit(solution)/shard_map/all_gather | solution.py:280
  186.4 570.9 %all-gather.9.cloned.1.call-start = ((), (), s32[]{:S(2)}) async-start(), calls=%async_computation.13 | async-start | bytes 1474560 | tf_op jit(solution)/shard_map/all_gather | solution.py:263
  262.1 590.2 %all-gather.17.cloned.1.call-start = ((), (), s32[]{:S(2)}) async-start(), calls=%async_computation.17 | async-start | bytes 5898240 | tf_op jit(solution)/shard_map/all_gather | solution.py:288
  285.8 189.9 %copy-start.62 = (bf16[14,14,64,1,1]{2,1,4,3,0:T(8,128)(2,1)}, bf16[14,14,64,1,1]{2,1,4,3,0:T(8,128)(2,1)S(1)}, u32[]{:S(2)}) copy-start(bf16[14,14,64,1,1]{2,1,4,3,0:T(8,128)(2,1)S(1)} %fusion.61) | copy-start | bytes 75268
  286.0 55.5 %copy-start.64 = (bf16[14,14,64]{2,1,0:T(8,128)(2,1)}, bf16[14,14,64]{2,1,0:T(8,128)(2,1)S(1)}, u32[]{:S(2)}) copy-start(bf16[14,14,64]{2,1,0:T(8,128)(2,1)S(1)} %convolution_convert_fusion) | copy-start | bytes 75268
  328.8 12.8 copy-start.8
  574.3 39.1 %copy-start.9 = (bf16[25,196,3,1,64]{1,0,4,3,2:T(8,128)(2,1)S(1)}, bf16[25,196,3,1,64]{1,0,4,3,2:T(8,128)(2,1)}, u32[]{:S(2)}) copy-start(bf16[25,196,3,1,64]{1,0,4,3,2:T(8,128)(2,1)} %copy-done.8) | copy-start | bytes 5644804
  638.2 9.8 copy-start.34
  638.2 9.8 copy-start.23
  648.0 10.2 copy-start.52
  670.0 27.9 %all-to-all-start.2 = ((bf16[4,1225,192]{1,2,0:T(8,128)(2,1)}), bf16[4,1225,192]{1,2,0:T(8,128)(2,1)S(1)}, u32[]{:S(2)}, u32[]{:S(2)}) async-start(bf16[4,1225,192]{1,2,0:T(8,128)(2,1)} %copy.237), calls=%async_computation.2 | async-start | bytes 3932160 | tf_op jit(solution)/shard_map/all_to_all | solution.py:106
  676.7 8.8 copy-start.76
  676.7 9.8 copy-start.40
  676.7 9.8 copy-start.81
  699.2 69.9 %all-to-all-start.6 = ((bf16[4,1225,192]{1,2,0:T(8,128)(2,1)}), bf16[4,1225,192]{1,2,0:T(8,128)(2,1)S(1)}, u32[]{:S(2)}, u32[]{:S(2)}) async-start(bf16[4,1225,192]{1,2,0:T(8,128)(2,1)} %copy.250), calls=%async_computation.6 | async-start | bytes 3932160 | tf_op jit(solution)/shard_map/all_to_all | solution.py:94
  702.8 188.7 %all-gather.13.cloned.1.call-start = ((), (), s32[]{:S(2)}) async-start(), calls=%async_computation.15 | async-start | bytes 5898240 | tf_op jit(solution)/shard_map/all_gather | solution.py:287
  769.1 53.3 %copy-start.11 = (bf16[4,1225,192]{1,2,0:T(8,128)(2,1)}, bf16[4,1225,192]{1,2,0:T(8,128)(2,1)S(1)}, u32[]{:S(2)}) copy-start(bf16[4,1225,192]{1,2,0:T(8,128)(2,1)S(1)} %all-to-all-done.6) | copy-start | bytes 5644804
  769.1 53.7 %all-to-all-start.3 = ((bf16[1225,4,192]{0,2,1:T(8,128)(2,1)}), bf16[1225,4,192]{0,2,1:T(8,128)(2,1)}, u32[]{:S(2)}, u32[]{:S(2)}) async-start(bf16[1225,4,192]{0,2,1:T(8,128)(2,1)} %bitcast.304), calls=%async_computation.3 | async-start | bytes 3932160 | tf_op jit(solution)/shard_map/all_to_all | solution.py:114
  781.5 9.8 copy-start.41
  781.5 10.0 copy-start.71
  791.3 149.7 %copy-start.54 = (bf16[1,3072,16]{1,2,0:T(8,128)(2,1)}, bf16[1,3072,16]{1,2,0:T(8,128)(2,1)S(1)}, u32[]{:S(2)}) copy-start(bf16[1,3072,16]{1,2,0:T(8,128)(2,1)S(1)} %copy.289) | copy-start | bytes 294916
  791.5 30.9 %copy-start.68 = (bf16[1,16,768]{2,0,1:T(2,128)(2,1)}, bf16[1,16,768]{2,0,1:T(2,128)(2,1)S(1)}, u32[]{:S(2)}) copy-start(bf16[1,16,768]{2,0,1:T(2,128)(2,1)S(1)} %fusion.121) | copy-start | bytes 73732
  822.7 118.3 %copy-start.60 = (f32[1225,16]{0,1:T(8,128)}, f32[1225,16]{0,1:T(8,128)S(1)}, u32[]{:S(2)}) copy-start(f32[1225,16]{0,1:T(8,128)S(1)} %fusion.118) | copy-start | bytes 235204
  847.5 29.2 %all-to-all-start.4 = ((bf16[4,1225,192]{1,2,0:T(8,128)(2,1)}), bf16[4,1225,192]{1,2,0:T(8,128)(2,1)}, u32[]{:S(2)}, u32[]{:S(2)}) async-start(bf16[4,1225,192]{1,2,0:T(8,128)(2,1)} %copy.244), calls=%async_computation.4 | async-start | bytes 3932160 | tf_op jit(solution)/shard_map/all_to_all | solution.py:94
  969.2 8.7 copy-start.36
  969.2 8.7 copy-start.7
  1032.5 29.3 %copy-start.67 = (bf16[1,16,768]{2,0,1:T(2,128)(2,1)S(1)}, bf16[1,16,768]{2,0,1:T(2,128)(2,1)}, u32[]{:S(2)}) copy-start(bf16[1,16,768]{2,0,1:T(2,128)(2,1)} %fusion.125) | copy-start | bytes 73732
  1033.9 27.9 %all-to-all-start.8 = ((bf16[4,1225,192]{1,2,0:T(8,128)(2,1)}), bf16[4,1225,192]{1,2,0:T(8,128)(2,1)S(1)}, u32[]{:S(2)}, u32[]{:S(2)}) async-start(bf16[4,1225,192]{1,2,0:T(8,128)(2,1)} %copy.253), calls=%async_computation.8 | async-start | bytes 3932160 | tf_op jit(solution)/shard_map/all_to_all | solution.py:106
  1072.6 15.0 slice-start
  1072.6 29.4 %all-to-all-start.9 = ((bf16[1225,4,192]{0,2,1:T(8,128)(2,1)}), bf16[1225,4,192]{0,2,1:T(8,128)(2,1)}, u32[]{:S(2)}, u32[]{:S(2)}) async-start(bf16[1225,4,192]{0,2,1:T(8,128)(2,1)} %bitcast.305), calls=%async_computation.9 | async-start | bytes 3932160 | tf_op jit(solution)/shard_map/all_to_all | solution.py:110
  1077.7 10.0 slice-start.1
  1077.7 10.0 copy-start.55
  1102.0 358.3 %all-to-all-start.5 = ((bf16[1225,4,192]{0,2,1:T(8,128)(2,1)}), bf16[1225,4,192]{0,2,1:T(8,128)(2,1)}, u32[]{:S(2)}, u32[]{:S(2)}) async-start(bf16[1225,4,192]{0,2,1:T(8,128)(2,1)} %bitcast.38), calls=%async_computation.5 | async-start | bytes 3932160 | tf_op jit(solution)/shard_map/all_to_all | solution.py:100
  1153.3 14.2 copy-start.10
  1267.6 94.8 %copy-start.65 = (bf16[14,14,64]{2,1,0:T(8,128)(2,1)S(1)}, bf16[14,14,64]{2,1,0:T(8,128)(2,1)}, u32[]{:S(2)}) copy-start(bf16[14,14,64]{2,1,0:T(8,128)(2,1)} %copy-done.64) | copy-start | bytes 75268
  1362.3 10.0 copy-start.14
  1362.3 10.0 copy-start.63
  1460.3 8.7 copy-start.39
  1460.3 17.3 slice-start.2
  1460.3 72.1 %all-to-all-start.10 = ((bf16[4,1225,576]{1,2,0:T(8,128)(2,1)}), bf16[4,1225,576]{1,2,0:T(8,128)(2,1)}, u32[]{:S(2)}, u32[]{:S(2)}) async-start(bf16[4,1225,576]{1,2,0:T(8,128)(2,1)} %copy.267), calls=%async_computation.10 | async-start | bytes 11796480 | tf_op jit(solution)/shard_map/all_to_all | solution.py:106
  1489.7 10.0 copy-start.19
  1489.7 10.0 copy-start.47
  1495.5 37.0 %copy-start.51 = (bf16[1,16,2304]{2,0,1:T(2,128)(2,1)S(1)}, bf16[1,16,2304]{2,0,1:T(2,128)(2,1)}, u32[]{:S(2)}) copy-start(bf16[1,16,2304]{2,0,1:T(2,128)(2,1)} %copy-done.50) | copy-start | bytes 221188
  1546.5 8.8 copy-start.16
  1550.7 33.6 %all-to-all-start.11 = ((bf16[1225,4,192]{0,2,1:T(8,128)(2,1)}), bf16[1225,4,192]{0,2,1:T(8,128)(2,1)}, u32[]{:S(2)}, u32[]{:S(2)}) async-start(bf16[1225,4,192]{0,2,1:T(8,128)(2,1)} %bitcast.303), calls=%async_computation.11 | async-start | bytes 3932160 | tf_op jit(solution)/shard_map/all_to_all | solution.py:114
  1555.2 174.2 %all-reduce.6.cloned.1.call-start = ((), (), s32[]{:S(2)}) async-start(), calls=%async_computation.18 | async-start | bytes 12582912 | tf_op jit(solution)/shard_map/psum | solution.py:338
  1613.2 130.1 %copy-start.1 = (bf16[27,64]{1,0:T(8,128)(2,1)S(1)}, bf16[27,64]{1,0:T(8,128)(2,1)}, u32[]{:S(2)}) copy-start(bf16[27,64]{1,0:T(8,128)(2,1)} %param.28) | copy-start | bytes 10372
  (50 other events, 279.4 us)
Sparse Core Ops, SparseCore 0:
  20.2 78.6 all-gather.6
  100.4 20.6 all-gather.14
  188.0 24.5 all-gather.10
  262.3 29.7 all-gather.8
  293.5 88.5 all-gather.16
  757.4 100.3 all-gather.12
  1566.8 162.6 all-reduce.5
